TPU v7x, 512 devices: a whole 4x8x8 slice. The times are simulated.
512 devices in a mesh: dom: 32 (over x, y_hi, core), bucket: 8 (over z), depth: 2 (over y_lo).
Axes of the slice: x: 4, y: 8 (y_hi: 4, y_lo: 2; y = y_hi * 2 + y_lo), z: 8, core: 2. Of those that a mesh axis runs over, the one named last changes fastest.
Arguments:
- entities: float32 [262144, 400], P(('dom', 'bucket')), may hold values from -7 to 7
- entity_state: float32 [262144], P(('dom', 'bucket')), may hold values from 0.05 to 0.5
- relations: float32 [256, 400], replicated, may hold values from 0.5 to 2
- relation_state: float32 [256], replicated, may hold values from 0.05 to 0.5
- edge_ends: int32 [2, 262144], P(None, ('dom', 'bucket')), may hold values from 0 to 1023
- relation_ids: int32 [262144], P(('dom', 'bucket')), may hold values from 0 to 255
- neg_ids: int32 [512, 1024], P(('dom', 'bucket'), 'depth'), may hold values from 0 to 1023
- edge_count: int32 [256], P(('dom', 'bucket')), may hold values from 16 to 1024, as said below
Outputs:
- new_entities: float32 [262144, 400], P(('dom', 'bucket'))
- new_state: float32 [262144], P(('dom', 'bucket'))
- new_relations: float32 [256, 400], replicated
Inputs may be any that keep to these rules, and one draw needn't show every extreme that they name: `edge_count`: the live slots of a partition are its first ones; partition 0 is full in every draw.
All inputs are finite; a program needn't handle non-finite values.
Results may differ from a plain program's by a relative error of at most 0.0006.
The roundings to bfloat16 on the way count: a program that leaves them out, or rounds other values in their place, can miss the bound.
Values may be sent and summed in bfloat16 or wider, within the bound.
No kernel may reach another device: no remote copies, remote signals or barrier semaphores. Data moves between devices by JAX's collectives and lax.ppermute only.
A program may use at most 64 MiB of HBM per device.

v0:
```python
import jax
import jax.numpy as jnp
from jax import lax
from jax.experimental import pallas as pl
from jax.experimental.pallas import tpu as pltpu
from jax.sharding import PartitionSpec as P

BLOCK = 512


entity_rate = 0.1
relation_rate = 1.0

F32 = jnp.float32
BF16 = jnp.bfloat16
NN = (((1,), (0,)), ((), ()))
NT = (((1,), (1,)), ((), ()))


def mm(a, b, dims=NN):
    return lax.dot_general(a, b, dims, preferred_element_type=F32)


def onehot(ids, rows):
    index = lax.broadcasted_iota(jnp.int32, (rows, ids.shape[1]), 0)
    return jnp.where(index == ids, 1.0, 0.0).astype(BF16)


def split(value, parts):
    out = []
    for _ in range(parts):
        piece = value.astype(BF16)
        out.append(piece)
        value = value - piece.astype(F32)
    return out


def prepare(entities, rel, ends, rid, neg_a, neg_b, q, left, scale, count):
    own = entities[...].astype(BF16)
    rel_parts = split(rel[...], 3)
    ones = jnp.ones((neg_a.shape[1], 128), BF16)
    for c in range(q.shape[1] // BLOCK):
        lanes = slice(c * BLOCK, (c + 1) * BLOCK)
        picked = mm(own, onehot(ends[0:1, lanes], own.shape[1]))
        by_rel = onehot(rid[0:1, lanes], rel.shape[1])
        factor = sum(mm(part, by_rel) for part in rel_parts)
        q[:, lanes] = (picked * factor).astype(BF16)
        left[:, lanes] = picked.astype(BF16)
        scale[:, lanes] = factor
        hits = mm(onehot(neg_a[c : c + 1, :], own.shape[1]), ones)
        count[c] = hits + mm(onehot(neg_b[c : c + 1, :], own.shape[1]), ones)


CHUNK = 512
TILE = 256


def block_lanes(block):
    return pl.ds(pl.multiple_of(block * BLOCK, BLOCK), BLOCK)


def softmax_coef(scores, times, right_ids, first, live):
    right = lax.broadcasted_iota(jnp.int32, scores.shape, 0) == right_ids
    positive = jnp.sum(jnp.where(right, scores, 0.0), axis=0, keepdims=True)
    masked = jnp.where(times > 0.0, scores, -3.0e38)
    peak = jnp.maximum(positive, jnp.max(masked, axis=0, keepdims=True))
    shifted = jnp.exp(masked - peak)
    top = jnp.exp(positive - peak)
    denom = top + jnp.sum(shifted * times, axis=0, keepdims=True)
    slot = lax.broadcasted_iota(jnp.int32, right_ids.shape, 1) + first
    active = jnp.where(slot < live, 1.0, 0.0)
    pos_coef = active * (top / denom - 1.0)
    weights = (shifted * (active / denom)).astype(BF16).astype(F32) * times
    return split(weights + jnp.where(right, pos_coef, 0.0), 2)


def own_block(
    block, live, ends, rid, outer, middle, peer, q, left, scale, count,
    high_hbm, low_hbm, grad_hbm, rel_hbm, far_hbm,
    high, low, grad, rel_grad, far, sems,
):
    edge, rest = outer.shape[1], far.shape[1] - outer.shape[1]
    far[:, pl.ds(pl.multiple_of(block[0] * rest, edge), edge)] = outer[...]
    far[:, edge:rest] = middle[...]
    far[:, pl.ds(pl.multiple_of((1 - block[0]) * rest, edge), edge)] = peer[...]
    keep = pltpu.make_async_copy(far, far_hbm, sems.at[3 * (BLOCK // CHUNK) + 1])
    keep.start()
    far_rows = far[...].T
    times = jnp.tile(count[block[0]], (1, CHUNK // 128))
    total, writes = None, [keep]
    for c in range(BLOCK // CHUNK):
        part = slice(c * CHUNK, (c + 1) * CHUNK)
        first = pl.multiple_of(block[0] * BLOCK + c * CHUNK, CHUNK)
        ids = pl.ds(first, CHUNK)
        scores = mm(far_rows, q[:, ids])
        upper, lower = softmax_coef(scores, times, ends[1:2, ids], first, live[0])
        high[:, part] = upper
        low[:, part] = lower
        query_grad = mm(far[...], upper) + mm(far[...], lower)
        grad[:, part] = (query_grad * scale[:, ids]).astype(BF16)
        for i, (src, dst) in enumerate([(high, high_hbm), (low, low_hbm), (grad, grad_hbm)]):
            write = pltpu.make_async_copy(
                src.at[:, part], dst.at[:, part], sems.at[3 * c + i]
            )
            write.start()
            writes.append(write)
        pieces = split(query_grad * left[:, ids].astype(F32), 2)
        by_rel = onehot(rid[0:1, ids], rel_grad.shape[0])
        share = mm(by_rel, pieces[0], NT) + mm(by_rel, pieces[1], NT)
        total = share if total is None else total + share
    rel_grad[...] = total
    write = pltpu.make_async_copy(rel_grad, rel_hbm, sems.at[3 * (BLOCK // CHUNK)])
    write.start()
    writes.append(write)
    for write in writes:
        write.wait()


def dithered(value):
    row = lax.broadcasted_iota(jnp.int32, (value.shape[0], 1), 0).astype(F32) * 0.61803398875
    shift = (row - jnp.floor(row) - 0.5) * (1.0 / 256.0)
    return (value + value * shift).astype(BF16)


def other_block(
    block, live, ends, far_hbm, q_hbm, scale_hbm, count_hbm, high_hbm, low_hbm,
    far_grad, grad,
    far, q, scale, count, high, low, sems,
):
    lanes = block_lanes(1 - block[0])
    done = block_lanes(block[0])
    reads = [
        pltpu.make_async_copy(src, dst, sems.at[i])
        for i, (src, dst) in enumerate(
            [
                (far_hbm, far),
                (q_hbm, q),
                (count_hbm.at[1 - block[0]], count),
                (scale_hbm.at[:, lanes], scale),
                (high_hbm, high.at[:, done]),
                (low_hbm, low.at[:, done]),
            ]
        )
    ]
    for read in reads:
        read.start()
    for read in reads[:4]:
        read.wait()
    far_rows = far[...].T
    times = jnp.tile(count[...], (1, CHUNK // 128))
    for c in range(BLOCK // CHUNK):
        first = pl.multiple_of((1 - block[0]) * BLOCK + c * CHUNK, CHUNK)
        ids = pl.ds(first, CHUNK)
        scores = mm(far_rows, q[:, ids])
        upper, lower = softmax_coef(scores, times, ends[1:2, ids], first, live[0])
        high[:, ids] = upper
        low[:, ids] = lower
        query_grad = mm(far[...], upper) + mm(far[...], lower)
        part = slice(c * CHUNK, (c + 1) * CHUNK)
        grad[:, part] = (query_grad * scale[:, part]).astype(BF16)
    for read in reads[4:]:
        read.wait()
    for c in range(far_grad.shape[1] // TILE):
        part = slice(c * TILE, (c + 1) * TILE)
        both = mm(q[...], high[part, :], NT) + mm(q[...], low[part, :], NT)
        far_grad[:, part] = dithered(both)


def update_entities(
    block, ends, state, home, ent_hbm, grad_a, grad_b, new_state, new_hbm,
    ent, grad, new, sems,
):
    reads = [
        pltpu.make_async_copy(src, dst, sems.at[i])
        for i, (src, dst) in enumerate(
            [
                (grad_a, grad.at[:, block_lanes(block[0])]),
                (grad_b, grad.at[:, block_lanes(1 - block[0])]),
                (ent_hbm, ent),
            ]
        )
    ]
    for read in reads:
        read.start()
    for read in reads:
        read.wait()
    writes = []
    for c in range(ent.shape[1] // TILE):
        part = slice(c * TILE, (c + 1) * TILE)
        index = lax.broadcasted_iota(jnp.int32, (TILE, ends.shape[1]), 0) + c * TILE
        chosen = jnp.where(index == ends[0:1, :], 1.0, 0.0).astype(BF16)
        total = mm(grad[...], chosen, NT) + home[:, part].astype(F32)
        updated = state[0:1, part] + jnp.mean(total * total, axis=0, keepdims=True)
        new_state[0:1, part] = updated
        new[:, part] = ent[:, part] - entity_rate * total / jnp.sqrt(updated)
        write = pltpu.make_async_copy(new.at[:, part], new_hbm.at[:, part], sems.at[3 + c])
        write.start()
        writes.append(write)
    for write in writes:
        write.wait()


def sum_spread(pieces, out):
    out[...] = jnp.broadcast_to(jnp.sum(pieces[...], axis=0, keepdims=True), out.shape)


def update_relations(pieces, rel, state, out):
    total = jnp.sum(pieces[...], axis=0)
    updated = state[...] + jnp.mean(total * total, axis=1, keepdims=True)
    new = rel[...] - relation_rate * total / jnp.sqrt(updated)
    out[...] = jnp.broadcast_to(new[None], out.shape)


def call(kernel, args, outs, spaces, out_spaces, scratch=()):
    def spec(space, shape):
        if space == "b":
            return pl.BlockSpec(shape, lambda: (0,) * len(shape))
        return pl.BlockSpec(memory_space={"s": pltpu.SMEM, "v": pltpu.VMEM, "h": pltpu.HBM}[space])

    args = [
        pltpu.with_memory_space_constraint(arg, pltpu.HBM) if space in "hb" else arg
        for space, arg in zip(spaces, args, strict=True)
    ]
    return pl.pallas_call(
        kernel,
        out_shape=[
            pltpu.HBM(out.shape, out.dtype) if space in "hb" else out
            for space, out in zip(out_spaces, outs, strict=True)
        ],
        in_specs=[spec(space, arg.shape) for space, arg in zip(spaces, args, strict=True)],
        out_specs=[spec(space, out.shape) for space, out in zip(out_spaces, outs, strict=True)],
        scratch_shapes=list(scratch),
        compiler_params=pltpu.CompilerParams(vmem_limit_bytes=24 << 20),
    )(*args)


def passed_along(block, axis, distance):
    size = lax.axis_size(axis)
    return lax.ppermute(block, axis, [((i - distance) % size, i) for i in range(size)])


def mesh_groups():
    n_bucket, n_depth = lax.axis_size("bucket"), lax.axis_size("depth")
    n_x, n_y, n_core = 4, lax.axis_size("dom") // 8, 2

    def dom(x, y, core):
        return (x * n_y + y) * n_core + core

    along = [
        [dom(x, y, core) * n_bucket + z for y in range(n_y) for z in range(n_bucket)]
        for x in range(n_x)
        for core in range(n_core)
    ]
    across = [
        [
            dom(x, y, core) * n_depth + k
            for x in range(n_x)
            for core in range(n_core)
            for k in range(n_depth)
        ]
        for y in range(n_y)
    ]
    place = (lax.axis_index("dom") // n_core % n_y) * n_bucket + lax.axis_index("bucket")
    return along, across, place


def local(
    entities, entity_state, relations, relation_state, edge_ends, relation_ids, neg_ids, edge_count
):
    half_dom = lax.axis_size("dom") // 2
    rows, width = entities.shape
    n_rel = relations.shape[0]
    edges = relation_ids.shape[0]
    shape = jax.ShapeDtypeStruct
    rid = relation_ids.reshape(1, edges)

    neg_other = passed_along(neg_ids, "depth", 1)
    depth = lax.axis_index("depth").astype(jnp.int32)
    edge = rows // 4
    outer = lax.dynamic_slice_in_dim(entities.T, depth * (rows - edge), edge, 1).astype(BF16)
    outer = passed_along(outer, "dom", half_dom)
    middle = entities.T[:, edge : rows - edge].astype(BF16)
    middle = passed_along(middle, "dom", half_dom)
    peer = passed_along(outer, "depth", 1)
    own, outer = lax.optimization_barrier((entities.T, outer))

    blocks = neg_ids.shape[0]
    wide, narrow = (width, edges), (width, BLOCK)
    q, left, scale, count = call(
        prepare,
        (own, relations.T, edge_ends, rid, neg_ids, neg_other),
        (shape(wide, BF16), shape(wide, BF16), shape(wide, F32), shape((blocks, rows, 128), F32)),
        "bbbbbv",
        "vvvv",
    )
    mine = depth.reshape(1)
    mat = (rows, BLOCK)
    high, low, grad_a, rel_grad, far = call(
        own_block,
        (mine, edge_count, edge_ends, rid, outer, middle, peer, q, left, scale, count),
        (
            shape(mat, BF16),
            shape(mat, BF16),
            shape(narrow, BF16),
            shape((n_rel, width), F32),
            shape((width, rows), BF16),
        ),
        "ssvvvvvvvvv",
        "hhhhh",
        (
            pltpu.VMEM(mat, BF16),
            pltpu.VMEM(mat, BF16),
            pltpu.VMEM(narrow, BF16),
            pltpu.VMEM((n_rel, width), F32),
            pltpu.VMEM((width, rows), BF16),
            pltpu.SemaphoreType.DMA((3 * (BLOCK // CHUNK) + 2,)),
        ),
    )
    along, across, place = mesh_groups()
    groups = len(along[0])
    share = n_rel // groups

    def exchange(pieces, axis, index_groups):
        return lax.all_to_all(pieces, axis, 0, 0, axis_index_groups=index_groups)

    pieces = exchange(rel_grad.reshape(groups, share, width), ("dom", "bucket"), along)

    far_grad, grad_b = call(
        other_block,
        (mine, edge_count, edge_ends, far, q, scale, count, high, low),
        (shape((width, rows), BF16), shape(narrow, BF16)),
        "ssvhhhhhh",
        "vb",
        (
            pltpu.VMEM((width, rows), BF16),
            pltpu.VMEM(wide, BF16),
            pltpu.VMEM(narrow, F32),
            pltpu.VMEM((rows, 128), F32),
            pltpu.VMEM((rows, edges), BF16),
            pltpu.VMEM((rows, edges), BF16),
            pltpu.SemaphoreType.DMA((6,)),
        ),
    )
    home_grad = passed_along(far_grad, "dom", half_dom)

    first = place * share
    my_rel = lax.dynamic_slice_in_dim(relations, first, share, 0)
    my_state = lax.dynamic_slice_in_dim(relation_state, first, share, 0)[:, None]
    pieces, far_grad = lax.optimization_barrier((pieces, far_grad))
    stack = (shape((len(across[0]), share, width), F32),)
    (partial,) = call(sum_spread, (pieces,), stack, "v", "b")
    totals = exchange(partial, ("dom", "depth"), across)
    stack = (shape((groups, share, width), F32),)
    (new_rel,) = call(update_relations, (totals, my_rel, my_state), stack, "vvv", "b")
    new_relations = exchange(new_rel, ("dom", "bucket"), along).reshape(n_rel, width)

    new_state, new_entities = call(
        update_entities,
        (mine, edge_ends, entity_state.reshape(1, rows), home_grad, entities.T, grad_a, grad_b),
        (shape((1, rows), F32), shape((width, rows), F32)),
        "svvvhhh",
        "vh",
        (
            pltpu.VMEM((width, rows), F32),
            pltpu.VMEM(wide, BF16),
            pltpu.VMEM((width, rows), F32),
            pltpu.SemaphoreType.DMA((7,)),
        ),
    )
    return (new_entities.T, new_state.reshape(rows), new_relations)


def solution(mesh):
    return jax.shard_map(
        local,
        mesh=mesh,
        in_specs=(
            P(("dom", "bucket"), None),
            P(("dom", "bucket")),
            P(),
            P(),
            P(None, ("dom", "bucket")),
            P(("dom", "bucket")),
            P(("dom", "bucket"), "depth"),
            P(("dom", "bucket")),
        ),
        out_specs=(P(("dom", "bucket"), None), P(("dom", "bucket")), P()),
        check_vma=False,
    )
```

profile of v0, /device:TPU:8, one launch (start us, length us, event | category | flops | bytes accessed | tf_op | source)
XLA Modules:
  0.0 103.0 jit_solution(16590439017843961540)
XLA Ops:
  0.6 0.0 copy-start
  0.7 0.0 copy-start.4
  0.7 0.0 copy-start.5
  0.7 1.0 %fusion = bf16[400,256]{1,0:T(8,128)(2,1)S(1)} fusion(f32[1024,400]{0,1:T(8,128)} %param.8, s32[]{:T(128)S(6)} %select_n.18), kind=kLoop, calls=%fused_computation.2 | loop fusion | bytes 409604 | tf_op jit(solution)/shard_map/convert_element_type | solution.py:280
  1.7 4.9 %collective-permute-start = (bf16[400,256]{1,0:T(8,128)(2,1)S(1)}, bf16[400,256]{1,0:T(8,128)(2,1)S(1)}, u32[]{:S(2)}, u32[]{:S(2)}) collective-permute-start(bf16[400,256]{1,0:T(8,128)(2,1)S(1)} %fusion), channel_id=1, source_target_pairs={{256,0},{272,16},{288,32},{304,48},{320,64},{336,80},{352,96},{368... | collective-permute-start | bytes 614408 | tf_op jit(solution)/shard_map/ppermute | solution.py:239
  6.7 1.2 %slice.7 = bf16[400,512]{1,0:T(8,128)(2,1)S(1)} slice(f32[400,1024]{1,0:T(8,128)} %bitcast.16), slice={[0:400], [256:768]} | slice | bytes 819200 | tf_op jit(solution)/shard_map/slice | solution.py:282
  7.9 2.4 %collective-permute-start.1 = (bf16[400,512]{1,0:T(8,128)(2,1)S(1)}, bf16[400,512]{1,0:T(8,128)(2,1)S(1)}, u32[]{:S(2)}, u32[]{:S(2)}) collective-permute-start(bf16[400,512]{1,0:T(8,128)(2,1)S(1)} %slice.7), channel_id=1, source_target_pairs={{256,0},{272,16},{288,32},{304,48},{320,64},{336,80},{352,96},{368... | collective-permute-start | bytes 1228808 | tf_op jit(solution)/shard_map/ppermute | solution.py:239
  10.3 1.7 %collective-permute-done.outer = bf16[400,256]{1,0:T(8,128)(2,1)S(1)} collective-permute-done((bf16[400,256]{1,0:T(8,128)(2,1)S(1)}, bf16[400,256]{1,0:T(8,128)(2,1)S(1)}, u32[]{:S(2)}, u32[]{:S(2)}) %collective-permute-start) | collective-permute-done | bytes 204832 | tf_op jit(solution)/shard_map/ppermute | solution.py:239
  12.0 8.7 %collective-permute-start.2 = (bf16[400,256]{1,0:T(8,128)(2,1)S(1)}, bf16[400,256]{1,0:T(8,128)(2,1)S(1)}, u32[]{:S(2)}, u32[]{:S(2)}) collective-permute-start(bf16[400,256]{1,0:T(8,128)(2,1)S(1)} %collective-permute-done.outer), channel_id=1, source_target_pairs={{1,0},{0,1},{3,2},{2,3},{5,4},{4,5},{7,6},{6,7},{9,8},{8,9},{11,10... | collective-permute-start | bytes 614408 | tf_op jit(solution)/shard_map/ppermute | solution.py:239
  20.8 1.9 %collective-permute-start.3 = (s32[2,512]{1,0:T(2,128)}, s32[2,512]{1,0:T(2,128)S(1)}, u32[]{:S(2)}, u32[]{:S(2)}) collective-permute-start(s32[2,512]{1,0:T(2,128)} %neg_a.1), channel_id=1, source_target_pairs={{1,0},{0,1},{3,2},{2,3},{5,4},{4,5},{7,6},{6,7},{9,8},{8,9},{11,10... | collective-permute-start | bytes 12296 | tf_op jit(solution)/shard_map/ppermute | solution.py:239
  23.3 3.1 %collective-permute-done.3.neg_b = s32[2,512]{1,0:T(2,128)S(1)} collective-permute-done((s32[2,512]{1,0:T(2,128)}, s32[2,512]{1,0:T(2,128)S(1)}, u32[]{:S(2)}, u32[]{:S(2)}) %collective-permute-start.3) | collective-permute-done | bytes 4128 | tf_op jit(solution)/shard_map/ppermute | solution.py:239
  26.5 4.4 %shard_map.103 = (bf16[400,1024]{1,0:T(8,128)(2,1)S(1)}, bf16[400,1024]{1,0:T(8,128)(2,1)S(1)}, f32[400,1024]{1,0:T(8,128)S(1)}, f32[2,1024,128]{2,1,0:T(8,128)S(1)}) custom-call(f32[400,1024]{1,0:T(8,128)} %bitcast.17, f32[400,256]{1,0:T(8,128)} %bitcast.20, s32[2,1024]{1,0:T(2,128)} %ends.7, s32[1,1024]{1,0:T(1,128)} %bitcast.13, s32[2,512]{1,0:T(2,128)} %neg_a.1, ...), custom_call_target="tpu_custom_call" | custom-call | tf_op jit(solution)/shard_map/pallas_call | solution.py:224
  30.8 0.0 copy-start.1
  30.8 0.0 copy-start.2
  30.9 0.0 copy-start.3
  30.9 0.0 collective-permute-done.2.peer
  30.9 0.0 collective-permute-done.1.middle
  30.9 0.0 copy-done.4
  30.9 0.0 copy-done.5
  30.9 4.6 %shard_map.104 = (bf16[1024,512]{1,0:T(8,128)(2,1)}, bf16[1024,512]{1,0:T(8,128)(2,1)}, bf16[400,512]{1,0:T(8,128)(2,1)}, f32[256,400]{1,0:T(8,128)}, bf16[400,1024]{1,0:T(8,128)(2,1)}) custom-call(s32[1]{0:T(128)} %bitcast.block, s32[1]{0:T(128)S(6)} %copy.15.live, s32[2,1024]{1,0:T(2,128)S(1)} %copy-done.4, s32[1,1024]{1,0:T(1,128)S(1)} %bitcast.14, ...), custom_call_target="tpu_custom_call" | custom-call | tf_op jit(solution)/shard_map/pallas_call | solution.py:224
  35.5 0.0 copy-done.1
  35.5 0.0 copy-done.2
  35.5 0.0 copy-done.3
  35.5 9.6 %all-to-all-start = ((f32[32,8,400]{2,1,0:T(8,128)}), f32[32,8,400]{2,1,0:T(8,128)S(1)}, u32[]{:S(2)}, u32[]{:S(2)}) async-start(f32[32,8,400]{2,1,0:T(8,128)} %bitcast.21), calls=%async_computation | async-start | bytes 1048576 | tf_op jit(solution)/shard_map/all_to_all | solution.py:324
  45.1 0.0 copy-start.7
  45.1 7.1 %shard_map.105 = (bf16[400,1024]{1,0:T(8,128)(2,1)S(1)}, bf16[400,512]{1,0:T(8,128)(2,1)}) custom-call(s32[1]{0:T(128)} %bitcast.block, s32[1]{0:T(128)S(6)} %copy.15.live, s32[2,1024]{1,0:T(2,128)S(1)} %copy-done.4, bf16[400,1024]{1,0:T(8,128)(2,1)} %get-tuple-element.25.far_hbm, bf16[400,1024]{1,0:T(8,128)(2,1)} %copy-done.3, f32[400,1024]{1,0:T(8,128)} %copy-done.1, ...), custom_call_target="tpu_custom_call" | custom-call | tf_op jit(solution)/shard_map/pallas_call | solution.py:224
  52.2 10.3 %all-to-all-done.pieces = f32[32,8,400]{2,1,0:T(8,128)S(1)} async-done(((f32[32,8,400]{2,1,0:T(8,128)}), f32[32,8,400]{2,1,0:T(8,128)S(1)}, u32[]{:S(2)}, u32[]{:S(2)}) %all-to-all-start) | async-done | bytes 409632 | tf_op jit(solution)/shard_map/all_to_all | solution.py:324
  62.5 0.8 shard_map.107
  63.3 0.0 copy-start.6
  63.3 5.6 %all-to-all-start.1 = ((f32[16,8,400]{2,1,0:T(8,128)}), f32[16,8,400]{2,1,0:T(8,128)S(1)}, u32[]{:S(2)}, u32[]{:S(2)}) async-start(f32[16,8,400]{2,1,0:T(8,128)} %shard_map.107), calls=%async_computation.1 | async-start | bytes 524288 | tf_op jit(solution)/shard_map/all_to_all | solution.py:324
  68.9 0.0 copy-done.7
  68.9 0.1 constant_dynamic-slice_fusion
  69.0 4.9 %collective-permute-start.4 = (bf16[400,1024]{1,0:T(8,128)(2,1)S(1)}, bf16[400,1024]{1,0:T(8,128)(2,1)S(1)}, u32[]{:S(2)}, u32[]{:S(2)}) collective-permute-start(bf16[400,1024]{1,0:T(8,128)(2,1)S(1)} %get-tuple-element.28), channel_id=1, source_target_pairs={{256,0},{272,16},{288,32},{304,48},{320,64},{336,80},{352,96},{368... | collective-permute-start | bytes 2457608 | tf_op jit(solution)/shard_map/ppermute | solution.py:239
  73.9 0.0 copy-done
  73.9 0.1 dynamic-slice_bitcast_fusion
  74.0 0.1 copy.14.rel
  74.1 0.1 copy.12.state
  74.2 1.6 %all-to-all-done.1.pieces = f32[16,8,400]{2,1,0:T(8,128)S(1)} async-done(((f32[16,8,400]{2,1,0:T(8,128)}), f32[16,8,400]{2,1,0:T(8,128)S(1)}, u32[]{:S(2)}, u32[]{:S(2)}) %all-to-all-start.1) | async-done | bytes 204832 | tf_op jit(solution)/shard_map/all_to_all | solution.py:324
  75.8 1.0 shard_map.108
  76.8 5.4 %all-to-all-start.2 = ((f32[32,8,400]{2,1,0:T(8,128)}), f32[32,8,400]{2,1,0:T(8,128)S(1)}, u32[]{:S(2)}, u32[]{:S(2)}) async-start(f32[32,8,400]{2,1,0:T(8,128)} %shard_map.108), calls=%async_computation.2 | async-start | bytes 1048576 | tf_op jit(solution)/shard_map/all_to_all | solution.py:324
  82.2 11.2 %collective-permute-done.4.home = bf16[400,1024]{1,0:T(8,128)(2,1)S(1)} collective-permute-done((bf16[400,1024]{1,0:T(8,128)(2,1)S(1)}, bf16[400,1024]{1,0:T(8,128)(2,1)S(1)}, u32[]{:S(2)}, u32[]{:S(2)}) %collective-permute-start.4) | collective-permute-done | bytes 819232 | tf_op jit(solution)/shard_map/ppermute | solution.py:239
  93.4 0.0 copy-done.6
  93.4 4.6 %shard_map.106 = (f32[1,1024]{1,0:T(1,128)}, f32[400,1024]{1,0:T(8,128)}) custom-call(s32[1]{0:T(128)} %bitcast.block, s32[2,1024]{1,0:T(2,128)S(1)} %copy-done.4, f32[1,1024]{1,0:T(1,128)S(1)} %bitcast.15, bf16[400,1024]{1,0:T(8,128)(2,1)S(1)} %collective-permute-done.4.home, f32[400,1024]{1,0:T(8,128)} %bitcast.18, ...), custom_call_target="tpu_custom_call" | custom-call | tf_op jit(solution)/shard_map/pallas_call | solution.py:224
  98.0 4.1 %all-to-all-done.2 = f32[32,8,400]{2,1,0:T(8,128)S(1)} async-done(((f32[32,8,400]{2,1,0:T(8,128)}), f32[32,8,400]{2,1,0:T(8,128)S(1)}, u32[]{:S(2)}, u32[]{:S(2)}) %all-to-all-start.2) | async-done | bytes 409632 | tf_op jit(solution)/shard_map/all_to_all | solution.py:324
  102.1 0.9 copy.13
Async XLA Ops:
  0.6 73.3 %copy-start = (f32[256]{0:T(256)S(1)}, f32[256]{0:T(256)}, u32[]{:S(2)}) copy-start(f32[256]{0:T(256)} %param.11) | copy-start | bytes 3076
  0.7 30.2 %copy-start.4 = (s32[2,1024]{1,0:T(2,128)S(1)}, s32[2,1024]{1,0:T(2,128)}, u32[]{:S(2)}) copy-start(s32[2,1024]{1,0:T(2,128)} %ends.7) | copy-start | bytes 24580
  0.7 30.2 %copy-start.5 = (s32[1024]{0:T(1024)S(1)}, s32[1024]{0:T(1024)}, u32[]{:S(2)}) copy-start(s32[1024]{0:T(1024)} %param.13) | copy-start | bytes 12292
  1.7 10.3 %collective-permute-start = (bf16[400,256]{1,0:T(8,128)(2,1)S(1)}, bf16[400,256]{1,0:T(8,128)(2,1)S(1)}, u32[]{:S(2)}, u32[]{:S(2)}) collective-permute-start(bf16[400,256]{1,0:T(8,128)(2,1)S(1)} %fusion), channel_id=1, source_target_pairs={{256,0},{272,16},{288,32},{304,48},{320,64},{336,80},{352,96},{368... | collective-permute-start | bytes 614408 | tf_op jit(solution)/shard_map/ppermute | solution.py:239
  7.9 23.0 %collective-permute-start.1 = (bf16[400,512]{1,0:T(8,128)(2,1)S(1)}, bf16[400,512]{1,0:T(8,128)(2,1)S(1)}, u32[]{:S(2)}, u32[]{:S(2)}) collective-permute-start(bf16[400,512]{1,0:T(8,128)(2,1)S(1)} %slice.7), channel_id=1, source_target_pairs={{256,0},{272,16},{288,32},{304,48},{320,64},{336,80},{352,96},{368... | collective-permute-start | bytes 1228808 | tf_op jit(solution)/shard_map/ppermute | solution.py:239
  12.0 18.9 %collective-permute-start.2 = (bf16[400,256]{1,0:T(8,128)(2,1)S(1)}, bf16[400,256]{1,0:T(8,128)(2,1)S(1)}, u32[]{:S(2)}, u32[]{:S(2)}) collective-permute-start(bf16[400,256]{1,0:T(8,128)(2,1)S(1)} %collective-permute-done.outer), channel_id=1, source_target_pairs={{1,0},{0,1},{3,2},{2,3},{5,4},{4,5},{7,6},{6,7},{9,8},{8,9},{11,10... | collective-permute-start | bytes 614408 | tf_op jit(solution)/shard_map/ppermute | solution.py:239
  20.8 5.7 %collective-permute-start.3 = (s32[2,512]{1,0:T(2,128)}, s32[2,512]{1,0:T(2,128)S(1)}, u32[]{:S(2)}, u32[]{:S(2)}) collective-permute-start(s32[2,512]{1,0:T(2,128)} %neg_a.1), channel_id=1, source_target_pairs={{1,0},{0,1},{3,2},{2,3},{5,4},{4,5},{7,6},{6,7},{9,8},{8,9},{11,10... | collective-permute-start | bytes 12296 | tf_op jit(solution)/shard_map/ppermute | solution.py:239
  30.8 4.6 %copy-start.1 = (f32[400,1024]{1,0:T(8,128)}, f32[400,1024]{1,0:T(8,128)S(1)}, u32[]{:S(2)}) copy-start(f32[400,1024]{1,0:T(8,128)S(1)} %get-tuple-element.23.scale.scale_hbm) | copy-start | bytes 4915204
  30.8 4.6 %copy-start.2 = (f32[2,1024,128]{2,1,0:T(8,128)}, f32[2,1024,128]{2,1,0:T(8,128)S(1)}, u32[]{:S(2)}) copy-start(f32[2,1024,128]{2,1,0:T(8,128)S(1)} %get-tuple-element.24.count.count_hbm) | copy-start | bytes 3145732
  30.9 4.6 %copy-start.3 = (bf16[400,1024]{1,0:T(8,128)(2,1)}, bf16[400,1024]{1,0:T(8,128)(2,1)S(1)}, u32[]{:S(2)}) copy-start(bf16[400,1024]{1,0:T(8,128)(2,1)S(1)} %get-tuple-element.21.q.q_hbm) | copy-start | bytes 2457604
  35.5 27.0 %all-to-all-start = ((f32[32,8,400]{2,1,0:T(8,128)}), f32[32,8,400]{2,1,0:T(8,128)S(1)}, u32[]{:S(2)}, u32[]{:S(2)}) async-start(f32[32,8,400]{2,1,0:T(8,128)} %bitcast.21), calls=%async_computation | async-start | bytes 1048576 | tf_op jit(solution)/shard_map/all_to_all | solution.py:324
  45.1 23.8 %copy-start.7 = (f32[256,400]{0,1:T(8,128)S(1)}, f32[256,400]{0,1:T(8,128)}, u32[]{:S(2)}) copy-start(f32[256,400]{0,1:T(8,128)} %param.10) | copy-start | bytes 1228804
  63.3 30.1 %copy-start.6 = (f32[1024]{0:T(1024)S(1)}, f32[1024]{0:T(1024)}, u32[]{:S(2)}) copy-start(f32[1024]{0:T(1024)} %param.9) | copy-start | bytes 12292
  63.3 12.5 %all-to-all-start.1 = ((f32[16,8,400]{2,1,0:T(8,128)}), f32[16,8,400]{2,1,0:T(8,128)S(1)}, u32[]{:S(2)}, u32[]{:S(2)}) async-start(f32[16,8,400]{2,1,0:T(8,128)} %shard_map.107), calls=%async_computation.1 | async-start | bytes 524288 | tf_op jit(solution)/shard_map/all_to_all | solution.py:324
  69.0 24.4 %collective-permute-start.4 = (bf16[400,1024]{1,0:T(8,128)(2,1)S(1)}, bf16[400,1024]{1,0:T(8,128)(2,1)S(1)}, u32[]{:S(2)}, u32[]{:S(2)}) collective-permute-start(bf16[400,1024]{1,0:T(8,128)(2,1)S(1)} %get-tuple-element.28), channel_id=1, source_target_pairs={{256,0},{272,16},{288,32},{304,48},{320,64},{336,80},{352,96},{368... | collective-permute-start | bytes 2457608 | tf_op jit(solution)/shard_map/ppermute | solution.py:239
  76.8 25.3 %all-to-all-start.2 = ((f32[32,8,400]{2,1,0:T(8,128)}), f32[32,8,400]{2,1,0:T(8,128)S(1)}, u32[]{:S(2)}, u32[]{:S(2)}) async-start(f32[32,8,400]{2,1,0:T(8,128)} %shard_map.108), calls=%async_computation.2 | async-start | bytes 1048576 | tf_op jit(solution)/shard_map/all_to_all | solution.py:324
where the time goes:
time: 104 us; the launch traced here: 103 us
  starting transfers between devices  43.5 us (42%)
  waiting for transfers between devices  32 us (31%)
  Pallas kernels  22.4 us (22%)
  local copies, waits for them, and re-layouts  3.57 us (3%)
  between operations  1.51 us (1%)
    ppermute x5, starting transfers between devices, passed_along(): lax.ppermute(block, axis, [((i - distance) % size, i) for i in range(size)])  22.9 us
    pallas_call x6, Pallas kernels, call(): pl.pallas_call(kernel, out_shape=[pltpu.HBM(out.shape, out.dtype) if spac...  22.4 us
    all_to_all x3, starting transfers between devices, exchange(): return lax.all_to_all(pieces, axis, 0, 0, axis_index_groups=index_groups)  20.6 us
    ppermute x5, waiting for transfers between devices, passed_along(): lax.ppermute(block, axis, [((i - distance) % size, i) for i in range(size)])  16 us
    all_to_all x3, waiting for transfers between devices, exchange(): return lax.all_to_all(pieces, axis, 0, 0, axis_index_groups=index_groups)  16 us
  transfers between devices with their start and end apart: 8, of which 6 were waited for; matrix products, arithmetic and copies ran while one was open for 2% of the time, Pallas kernels for 17%

commit v1 on v0

--- a/solution.py
+++ b/solution.py
@@ -35,20 +35,47 @@
     return out
 
 
-def prepare(entities, rel, ends, rid, neg_a, neg_b, q, left, scale, count):
-    own = entities[...].astype(BF16)
+def pack(depth, ent_hbm, outer, middle, own, ent, sems):
+    edge, half = outer.shape[1], middle.shape[1]
+    rest = own.shape[1] - edge
+    first = pl.ds(pl.multiple_of(depth[0] * rest, edge), edge)
+    last = pl.ds(pl.multiple_of((1 - depth[0]) * rest, edge), edge)
+    reads = [
+        pltpu.make_async_copy(ent_hbm.at[:, lanes], ent.at[:, lanes], sems.at[i])
+        for i, lanes in enumerate([first, pl.ds(edge, half), last])
+    ]
+    for read in reads:
+        read.start()
+    reads[0].wait()
+    piece = ent[:, first].astype(BF16)
+    outer[...] = piece
+    own[:, first] = piece
+    reads[1].wait()
+    piece = ent[:, edge:rest].astype(BF16)
+    middle[...] = piece
+    own[:, edge:rest] = piece
+    reads[2].wait()
+    own[:, last] = ent[:, last].astype(BF16)
+
+
+def prepare(own, ends, rid, neg_a, neg_b, rel_hbm, q, left, scale, count, rel, sems):
+    read = pltpu.make_async_copy(rel_hbm, rel, sems.at[0])
+    read.start()
+    ones = jnp.ones((neg_a.shape[1], 128), BF16)
+    blocks = q.shape[1] // BLOCK
+    for c in range(blocks):
+        hits = mm(onehot(neg_a[c : c + 1, :], own.shape[1]), ones)
+        count[c] = hits + mm(onehot(neg_b[c : c + 1, :], own.shape[1]), ones)
+    read.wait()
     rel_parts = split(rel[...], 3)
-    ones = jnp.ones((neg_a.shape[1], 128), BF16)
-    for c in range(q.shape[1] // BLOCK):
+    for c in range(blocks):
         lanes = slice(c * BLOCK, (c + 1) * BLOCK)
-        picked = mm(own, onehot(ends[0:1, lanes], own.shape[1]))
+        picked = mm(own[...], onehot(ends[0:1, lanes], own.shape[1]))
         by_rel = onehot(rid[0:1, lanes], rel.shape[1])
         factor = sum(mm(part, by_rel) for part in rel_parts)
         q[:, lanes] = (picked * factor).astype(BF16)
         left[:, lanes] = picked.astype(BF16)
         scale[:, lanes] = factor
-        hits = mm(onehot(neg_a[c : c + 1, :], own.shape[1]), ones)
-        count[c] = hits + mm(onehot(neg_b[c : c + 1, :], own.shape[1]), ones)
 
 
 CHUNK = 512
@@ -277,23 +304,30 @@
     neg_other = passed_along(neg_ids, "depth", 1)
     depth = lax.axis_index("depth").astype(jnp.int32)
     edge = rows // 4
-    outer = lax.dynamic_slice_in_dim(entities.T, depth * (rows - edge), edge, 1).astype(BF16)
+    mine = depth.reshape(1)
+    outer, middle, own = call(
+        pack,
+        (mine, entities.T),
+        (shape((width, edge), BF16), shape((width, rows - 2 * edge), BF16), shape((width, rows), BF16)),
+        "sh",
+        "vvv",
+        (pltpu.VMEM((width, rows), F32), pltpu.SemaphoreType.DMA((3,))),
+    )
     outer = passed_along(outer, "dom", half_dom)
-    middle = entities.T[:, edge : rows - edge].astype(BF16)
     middle = passed_along(middle, "dom", half_dom)
     peer = passed_along(outer, "depth", 1)
-    own, outer = lax.optimization_barrier((entities.T, outer))
+    own, outer = lax.optimization_barrier((own, outer))
 
     blocks = neg_ids.shape[0]
     wide, narrow = (width, edges), (width, BLOCK)
     q, left, scale, count = call(
         prepare,
-        (own, relations.T, edge_ends, rid, neg_ids, neg_other),
+        (own, edge_ends, rid, neg_ids, neg_other, relations.T),
         (shape(wide, BF16), shape(wide, BF16), shape(wide, F32), shape((blocks, rows, 128), F32)),
-        "bbbbbv",
+        "vvvvvh",
         "vvvv",
-    )
-    mine = depth.reshape(1)
+        (pltpu.VMEM((width, n_rel), F32), pltpu.SemaphoreType.DMA((1,))),
+    )
     mat = (rows, BLOCK)
     high, low, grad_a, rel_grad, far = call(
         own_block,

time: 104 us -> 102 us (0.981)
  local copies, waits for them, and re-layouts: 3.57 us -> 1.34 us
    slice x1 -> x0, local copies, waits for them, and re-layouts: 1.2 us -> none  [local(): middle = entities.T[:, edge:rows - edge].astype(BF16)]
    pallas_call x6 -> x7, Pallas kernels: 22.4 us -> 22.6 us  [call(): pl.pallas_call(kernel, out_shape=[pltpu.HBM(out.shape, out.dtype) if spac...]
  transfers between devices with their start and end apart: 8 -> 8, of which waited for: 6 -> 6; matrix products, arithmetic and copies ran while one was open for 2% -> 0% of each run, Pallas kernels for 17% -> 15%
where the time goes in v1:
time: 102 us
  starting transfers between devices  43.3 us (42%)
  waiting for transfers between devices  32.9 us (32%)
  Pallas kernels  22.6 us (22%)
  between operations  1.52 us (1%)
  local copies, waits for them, and re-layouts  1.34 us (1%)
    ppermute x5, starting transfers between devices, passed_along(): lax.ppermute(block, axis, [((i - distance) % size, i) for i in range(size)])  22.8 us
    pallas_call x7, Pallas kernels, call(): pl.pallas_call(kernel, out_shape=[pltpu.HBM(out.shape, out.dtype) if spac...  22.6 us
    all_to_all x3, starting transfers between devices, exchange(): return lax.all_to_all(pieces, axis, 0, 0, axis_index_groups=index_groups)  20.5 us
    ppermute x5, waiting for transfers between devices, passed_along(): lax.ppermute(block, axis, [((i - distance) % size, i) for i in range(size)])  16.9 us
    all_to_all x3, waiting for transfers between devices, exchange(): return lax.all_to_all(pieces, axis, 0, 0, axis_index_groups=index_groups)  16.1 us
  transfers between devices with their start and end apart: 8, of which 6 were waited for; matrix products, arithmetic and copies ran while one was open for 0% of the time, Pallas kernels for 15%

profile of v1, /device:TPU:8, one launch (start us, length us, event | category | flops | bytes accessed | tf_op | source)
XLA Modules:
  0.0 101.7 jit_solution(2188258896894227922)
XLA Ops:
  0.6 0.0 copy-start
  0.6 0.0 copy-start.6
  0.7 0.0 copy-start.5
  0.7 0.0 copy-start.4
  0.7 1.5 %shard_map.103 = (bf16[400,256]{1,0:T(8,128)(2,1)S(1)}, bf16[400,512]{1,0:T(8,128)(2,1)S(1)}, bf16[400,1024]{1,0:T(8,128)(2,1)S(1)}) custom-call(s32[1]{0:T(128)} %bitcast.depth.block, f32[400,1024]{1,0:T(8,128)} %bitcast.14), custom_call_target="tpu_custom_call" | custom-call | tf_op jit(solution)/shard_map/pallas_call | solution.py:251
  2.1 4.9 %collective-permute-start = (bf16[400,256]{1,0:T(8,128)(2,1)S(1)}, bf16[400,256]{1,0:T(8,128)(2,1)S(1)}, u32[]{:S(2)}, u32[]{:S(2)}) collective-permute-start(bf16[400,256]{1,0:T(8,128)(2,1)S(1)} %get-tuple-element.23), channel_id=1, source_target_pairs={{256,0},{272,16},{288,32},{304,48},{320,64},{336,80},{352,96},{368... | collective-permute-start | bytes 614408 | tf_op jit(solution)/shard_map/ppermute | solution.py:266
  7.1 2.4 %collective-permute-start.1 = (bf16[400,512]{1,0:T(8,128)(2,1)S(1)}, bf16[400,512]{1,0:T(8,128)(2,1)S(1)}, u32[]{:S(2)}, u32[]{:S(2)}) collective-permute-start(bf16[400,512]{1,0:T(8,128)(2,1)S(1)} %get-tuple-element.25), channel_id=1, source_target_pairs={{256,0},{272,16},{288,32},{304,48},{320,64},{336,80},{352,96},{368... | collective-permute-start | bytes 1228808 | tf_op jit(solution)/shard_map/ppermute | solution.py:266
  9.5 3.0 %collective-permute-done.outer = bf16[400,256]{1,0:T(8,128)(2,1)S(1)} collective-permute-done((bf16[400,256]{1,0:T(8,128)(2,1)S(1)}, bf16[400,256]{1,0:T(8,128)(2,1)S(1)}, u32[]{:S(2)}, u32[]{:S(2)}) %collective-permute-start) | collective-permute-done | bytes 204832 | tf_op jit(solution)/shard_map/ppermute | solution.py:266
  12.5 8.7 %collective-permute-start.2 = (bf16[400,256]{1,0:T(8,128)(2,1)S(1)}, bf16[400,256]{1,0:T(8,128)(2,1)S(1)}, u32[]{:S(2)}, u32[]{:S(2)}) collective-permute-start(bf16[400,256]{1,0:T(8,128)(2,1)S(1)} %collective-permute-done.outer), channel_id=1, source_target_pairs={{1,0},{0,1},{3,2},{2,3},{5,4},{4,5},{7,6},{6,7},{9,8},{8,9},{11,10... | collective-permute-start | bytes 614408 | tf_op jit(solution)/shard_map/ppermute | solution.py:266
  21.2 0.0 copy-done.6
  21.2 1.9 %collective-permute-start.3 = (s32[2,512]{1,0:T(2,128)S(1)}, s32[2,512]{1,0:T(2,128)S(1)}, u32[]{:S(2)}, u32[]{:S(2)}) collective-permute-start(s32[2,512]{1,0:T(2,128)S(1)} %copy-done.6), channel_id=1, source_target_pairs={{1,0},{0,1},{3,2},{2,3},{5,4},{4,5},{7,6},{6,7},{9,8},{8,9},{11,10... | collective-permute-start | bytes 12296 | tf_op jit(solution)/shard_map/ppermute | solution.py:266
  23.8 2.9 %collective-permute-done.3.neg_b = s32[2,512]{1,0:T(2,128)S(1)} collective-permute-done((s32[2,512]{1,0:T(2,128)S(1)}, s32[2,512]{1,0:T(2,128)S(1)}, u32[]{:S(2)}, u32[]{:S(2)}) %collective-permute-start.3) | collective-permute-done | bytes 4128 | tf_op jit(solution)/shard_map/ppermute | solution.py:266
  26.7 0.0 copy-done.5
  26.7 0.0 copy-done.4
  26.7 3.0 %shard_map.104 = (bf16[400,1024]{1,0:T(8,128)(2,1)S(1)}, bf16[400,1024]{1,0:T(8,128)(2,1)S(1)}, f32[400,1024]{1,0:T(8,128)S(1)}, f32[2,1024,128]{2,1,0:T(8,128)S(1)}) custom-call(bf16[400,1024]{1,0:T(8,128)(2,1)S(1)} %get-tuple-element.26.own, s32[2,1024]{1,0:T(2,128)S(1)} %copy-done.4, s32[1,1024]{1,0:T(1,128)S(1)} %bitcast.11, s32[2,512]{1,0:T(2,128)S(1)} %copy-done.6, ...), custom_call_target="tpu_custom_call" | custom-call | tf_op jit(solution)/shard_map/pallas_call | solution.py:251
  29.7 0.0 copy-start.1
  29.7 0.0 copy-start.2
  29.7 0.0 copy-start.3
  29.7 0.0 collective-permute-done.2.peer
  29.8 0.0 collective-permute-done.1.middle
  29.8 4.6 %shard_map.105 = (bf16[1024,512]{1,0:T(8,128)(2,1)}, bf16[1024,512]{1,0:T(8,128)(2,1)}, bf16[400,512]{1,0:T(8,128)(2,1)}, f32[256,400]{1,0:T(8,128)}, bf16[400,1024]{1,0:T(8,128)(2,1)}) custom-call(s32[1]{0:T(128)} %bitcast.depth.block, s32[1]{0:T(128)S(6)} %copy.15.live, s32[2,1024]{1,0:T(2,128)S(1)} %copy-done.4, s32[1,1024]{1,0:T(1,128)S(1)} %bitcast.12, ...), custom_call_target="tpu_custom_call" | custom-call | tf_op jit(solution)/shard_map/pallas_call | solution.py:251
  34.4 0.0 copy-done.1
  34.4 0.0 copy-done.2
  34.4 0.0 copy-done.3
  34.4 9.7 %all-to-all-start = ((f32[32,8,400]{2,1,0:T(8,128)}), f32[32,8,400]{2,1,0:T(8,128)S(1)}, u32[]{:S(2)}, u32[]{:S(2)}) async-start(f32[32,8,400]{2,1,0:T(8,128)} %bitcast.18), calls=%async_computation | async-start | bytes 1048576 | tf_op jit(solution)/shard_map/all_to_all | solution.py:358
  44.1 0.0 copy-start.8
  44.1 7.1 %shard_map.106 = (bf16[400,1024]{1,0:T(8,128)(2,1)S(1)}, bf16[400,512]{1,0:T(8,128)(2,1)}) custom-call(s32[1]{0:T(128)} %bitcast.depth.block, s32[1]{0:T(128)S(6)} %copy.15.live, s32[2,1024]{1,0:T(2,128)S(1)} %copy-done.4, bf16[400,1024]{1,0:T(8,128)(2,1)} %get-tuple-element.31.far_hbm, bf16[400,1024]{1,0:T(8,128)(2,1)} %copy-done.3, f32[400,1024]{1,0:T(8,128)} %copy-done.1, ...), custom_call_target="tpu_custom_call" | custom-call | tf_op jit(solution)/shard_map/pallas_call | solution.py:251
  51.3 10.2 %all-to-all-done.pieces = f32[32,8,400]{2,1,0:T(8,128)S(1)} async-done(((f32[32,8,400]{2,1,0:T(8,128)}), f32[32,8,400]{2,1,0:T(8,128)S(1)}, u32[]{:S(2)}, u32[]{:S(2)}) %all-to-all-start) | async-done | bytes 409632 | tf_op jit(solution)/shard_map/all_to_all | solution.py:358
  61.4 0.8 shard_map.108
  62.2 0.0 copy-start.7
  62.2 5.1 %all-to-all-start.1 = ((f32[16,8,400]{2,1,0:T(8,128)}), f32[16,8,400]{2,1,0:T(8,128)S(1)}, u32[]{:S(2)}, u32[]{:S(2)}) async-start(f32[16,8,400]{2,1,0:T(8,128)} %shard_map.108), calls=%async_computation.1 | async-start | bytes 524288 | tf_op jit(solution)/shard_map/all_to_all | solution.py:358
  67.3 0.0 copy-done.8
  67.3 0.1 constant_dynamic-slice_fusion
  67.4 4.9 %collective-permute-start.4 = (bf16[400,1024]{1,0:T(8,128)(2,1)S(1)}, bf16[400,1024]{1,0:T(8,128)(2,1)S(1)}, u32[]{:S(2)}, u32[]{:S(2)}) collective-permute-start(bf16[400,1024]{1,0:T(8,128)(2,1)S(1)} %get-tuple-element.34), channel_id=1, source_target_pairs={{256,0},{272,16},{288,32},{304,48},{320,64},{336,80},{352,96},{368... | collective-permute-start | bytes 2457608 | tf_op jit(solution)/shard_map/ppermute | solution.py:266
  72.3 0.0 copy-done
  72.3 0.1 dynamic-slice_bitcast_fusion
  72.4 0.1 copy.14.rel
  72.5 0.1 copy.12.state
  72.6 1.6 %all-to-all-done.1.pieces = f32[16,8,400]{2,1,0:T(8,128)S(1)} async-done(((f32[16,8,400]{2,1,0:T(8,128)}), f32[16,8,400]{2,1,0:T(8,128)S(1)}, u32[]{:S(2)}, u32[]{:S(2)}) %all-to-all-start.1) | async-done | bytes 204832 | tf_op jit(solution)/shard_map/all_to_all | solution.py:358
  74.2 1.0 %shard_map.109 = f32[32,8,400]{2,1,0:T(8,128)} custom-call(f32[16,8,400]{2,1,0:T(8,128)S(1)} %all-to-all-done.1.pieces, f32[8,400]{1,0:T(8,128)S(1)} %copy.14.rel, f32[8,1]{1,0:T(8,128)S(1)} %copy.12.state), custom_call_target="tpu_custom_call" | custom-call | tf_op jit(solution)/shard_map/pallas_call | solution.py:251
  75.2 5.7 %all-to-all-start.2 = ((f32[32,8,400]{2,1,0:T(8,128)}), f32[32,8,400]{2,1,0:T(8,128)S(1)}, u32[]{:S(2)}, u32[]{:S(2)}) async-start(f32[32,8,400]{2,1,0:T(8,128)} %shard_map.109), calls=%async_computation.2 | async-start | bytes 1048576 | tf_op jit(solution)/shard_map/all_to_all | solution.py:358
  80.9 10.9 %collective-permute-done.4.home = bf16[400,1024]{1,0:T(8,128)(2,1)S(1)} collective-permute-done((bf16[400,1024]{1,0:T(8,128)(2,1)S(1)}, bf16[400,1024]{1,0:T(8,128)(2,1)S(1)}, u32[]{:S(2)}, u32[]{:S(2)}) %collective-permute-start.4) | collective-permute-done | bytes 819232 | tf_op jit(solution)/shard_map/ppermute | solution.py:266
  91.8 0.0 copy-done.7
  91.8 4.6 %shard_map.107 = (f32[1,1024]{1,0:T(1,128)}, f32[400,1024]{1,0:T(8,128)}) custom-call(s32[1]{0:T(128)} %bitcast.depth.block, s32[2,1024]{1,0:T(2,128)S(1)} %copy-done.4, f32[1,1024]{1,0:T(1,128)S(1)} %bitcast.13, bf16[400,1024]{1,0:T(8,128)(2,1)S(1)} %collective-permute-done.4.home, f32[400,1024]{1,0:T(8,128)} %bitcast.15, ...), custom_call_target="tpu_custom_call" | custom-call | tf_op jit(solution)/shard_map/pallas_call | solution.py:251
  96.4 4.3 %all-to-all-done.2 = f32[32,8,400]{2,1,0:T(8,128)S(1)} async-done(((f32[32,8,400]{2,1,0:T(8,128)}), f32[32,8,400]{2,1,0:T(8,128)S(1)}, u32[]{:S(2)}, u32[]{:S(2)}) %all-to-all-start.2) | async-done | bytes 409632 | tf_op jit(solution)/shard_map/all_to_all | solution.py:358
  100.7 0.9 copy.13
Async XLA Ops:
  0.6 71.7 %copy-start = (f32[256]{0:T(256)S(1)}, f32[256]{0:T(256)}, u32[]{:S(2)}) copy-start(f32[256]{0:T(256)} %param.11) | copy-start | bytes 3076
  0.6 20.5 %copy-start.6 = (s32[2,512]{1,0:T(2,128)S(1)}, s32[2,512]{1,0:T(2,128)}, u32[]{:S(2)}) copy-start(s32[2,512]{1,0:T(2,128)} %neg_a.1) | copy-start | bytes 12292
  0.7 26.0 %copy-start.5 = (s32[1024]{0:T(1024)S(1)}, s32[1024]{0:T(1024)}, u32[]{:S(2)}) copy-start(s32[1024]{0:T(1024)} %param.13) | copy-start | bytes 12292
  0.7 26.0 %copy-start.4 = (s32[2,1024]{1,0:T(2,128)S(1)}, s32[2,1024]{1,0:T(2,128)}, u32[]{:S(2)}) copy-start(s32[2,1024]{1,0:T(2,128)} %ends.7) | copy-start | bytes 24580
  2.1 10.4 %collective-permute-start = (bf16[400,256]{1,0:T(8,128)(2,1)S(1)}, bf16[400,256]{1,0:T(8,128)(2,1)S(1)}, u32[]{:S(2)}, u32[]{:S(2)}) collective-permute-start(bf16[400,256]{1,0:T(8,128)(2,1)S(1)} %get-tuple-element.23), channel_id=1, source_target_pairs={{256,0},{272,16},{288,32},{304,48},{320,64},{336,80},{352,96},{368... | collective-permute-start | bytes 614408 | tf_op jit(solution)/shard_map/ppermute | solution.py:266
  7.1 22.7 %collective-permute-start.1 = (bf16[400,512]{1,0:T(8,128)(2,1)S(1)}, bf16[400,512]{1,0:T(8,128)(2,1)S(1)}, u32[]{:S(2)}, u32[]{:S(2)}) collective-permute-start(bf16[400,512]{1,0:T(8,128)(2,1)S(1)} %get-tuple-element.25), channel_id=1, source_target_pairs={{256,0},{272,16},{288,32},{304,48},{320,64},{336,80},{352,96},{368... | collective-permute-start | bytes 1228808 | tf_op jit(solution)/shard_map/ppermute | solution.py:266
  12.5 17.2 %collective-permute-start.2 = (bf16[400,256]{1,0:T(8,128)(2,1)S(1)}, bf16[400,256]{1,0:T(8,128)(2,1)S(1)}, u32[]{:S(2)}, u32[]{:S(2)}) collective-permute-start(bf16[400,256]{1,0:T(8,128)(2,1)S(1)} %collective-permute-done.outer), channel_id=1, source_target_pairs={{1,0},{0,1},{3,2},{2,3},{5,4},{4,5},{7,6},{6,7},{9,8},{8,9},{11,10... | collective-permute-start | bytes 614408 | tf_op jit(solution)/shard_map/ppermute | solution.py:266
  21.2 5.5 %collective-permute-start.3 = (s32[2,512]{1,0:T(2,128)S(1)}, s32[2,512]{1,0:T(2,128)S(1)}, u32[]{:S(2)}, u32[]{:S(2)}) collective-permute-start(s32[2,512]{1,0:T(2,128)S(1)} %copy-done.6), channel_id=1, source_target_pairs={{1,0},{0,1},{3,2},{2,3},{5,4},{4,5},{7,6},{6,7},{9,8},{8,9},{11,10... | collective-permute-start | bytes 12296 | tf_op jit(solution)/shard_map/ppermute | solution.py:266
  29.7 4.7 %copy-start.1 = (f32[400,1024]{1,0:T(8,128)}, f32[400,1024]{1,0:T(8,128)S(1)}, u32[]{:S(2)}) copy-start(f32[400,1024]{1,0:T(8,128)S(1)} %get-tuple-element.29.scale.scale_hbm) | copy-start | bytes 4915204
  29.7 4.7 %copy-start.2 = (f32[2,1024,128]{2,1,0:T(8,128)}, f32[2,1024,128]{2,1,0:T(8,128)S(1)}, u32[]{:S(2)}) copy-start(f32[2,1024,128]{2,1,0:T(8,128)S(1)} %get-tuple-element.30.count.count_hbm) | copy-start | bytes 3145732
  29.7 4.7 %copy-start.3 = (bf16[400,1024]{1,0:T(8,128)(2,1)}, bf16[400,1024]{1,0:T(8,128)(2,1)S(1)}, u32[]{:S(2)}) copy-start(bf16[400,1024]{1,0:T(8,128)(2,1)S(1)} %get-tuple-element.27.q.q_hbm) | copy-start | bytes 2457604
  34.4 27.0 %all-to-all-start = ((f32[32,8,400]{2,1,0:T(8,128)}), f32[32,8,400]{2,1,0:T(8,128)S(1)}, u32[]{:S(2)}, u32[]{:S(2)}) async-start(f32[32,8,400]{2,1,0:T(8,128)} %bitcast.18), calls=%async_computation | async-start | bytes 1048576 | tf_op jit(solution)/shard_map/all_to_all | solution.py:358
  44.1 23.2 %copy-start.8 = (f32[256,400]{0,1:T(8,128)S(1)}, f32[256,400]{0,1:T(8,128)}, u32[]{:S(2)}) copy-start(f32[256,400]{0,1:T(8,128)} %param.10) | copy-start | bytes 1228804
  62.2 29.6 %copy-start.7 = (f32[1024]{0:T(1024)S(1)}, f32[1024]{0:T(1024)}, u32[]{:S(2)}) copy-start(f32[1024]{0:T(1024)} %param.9) | copy-start | bytes 12292
  62.2 12.0 %all-to-all-start.1 = ((f32[16,8,400]{2,1,0:T(8,128)}), f32[16,8,400]{2,1,0:T(8,128)S(1)}, u32[]{:S(2)}, u32[]{:S(2)}) async-start(f32[16,8,400]{2,1,0:T(8,128)} %shard_map.108), calls=%async_computation.1 | async-start | bytes 524288 | tf_op jit(solution)/shard_map/all_to_all | solution.py:358
  67.4 24.4 %collective-permute-start.4 = (bf16[400,1024]{1,0:T(8,128)(2,1)S(1)}, bf16[400,1024]{1,0:T(8,128)(2,1)S(1)}, u32[]{:S(2)}, u32[]{:S(2)}) collective-permute-start(bf16[400,1024]{1,0:T(8,128)(2,1)S(1)} %get-tuple-element.34), channel_id=1, source_target_pairs={{256,0},{272,16},{288,32},{304,48},{320,64},{336,80},{352,96},{368... | collective-permute-start | bytes 2457608 | tf_op jit(solution)/shard_map/ppermute | solution.py:266
  75.2 25.5 %all-to-all-start.2 = ((f32[32,8,400]{2,1,0:T(8,128)}), f32[32,8,400]{2,1,0:T(8,128)S(1)}, u32[]{:S(2)}, u32[]{:S(2)}) async-start(f32[32,8,400]{2,1,0:T(8,128)} %shard_map.109), calls=%async_computation.2 | async-start | bytes 1048576 | tf_op jit(solution)/shard_map/all_to_all | solution.py:358

commit v2 on v1

--- a/solution.py
+++ b/solution.py
@@ -266,29 +266,30 @@
     return lax.ppermute(block, axis, [((i - distance) % size, i) for i in range(size)])
 
 
+AXES = ("dom", "bucket", "depth")
+
+
 def mesh_groups():
-    n_bucket, n_depth = lax.axis_size("bucket"), lax.axis_size("depth")
-    n_x, n_y, n_core = 4, lax.axis_size("dom") // 8, 2
-
-    def dom(x, y, core):
-        return (x * n_y + y) * n_core + core
-
-    along = [
-        [dom(x, y, core) * n_bucket + z for y in range(n_y) for z in range(n_bucket)]
+    n_z, n_k = lax.axis_size("bucket"), lax.axis_size("depth")
+    n_x, n_y, n_core, near = 4, lax.axis_size("dom") // 8, 2, 2
+
+    def device(x, y, core, high, low, k):
+        return (((x * n_y + y) * n_core + core) * n_z + high * near + low) * n_k + k
+
+    inside = [
+        (x, core, low, k)
         for x in range(n_x)
         for core in range(n_core)
+        for low in range(near)
+        for k in range(n_k)
     ]
-    across = [
-        [
-            dom(x, y, core) * n_depth + k
-            for x in range(n_x)
-            for core in range(n_core)
-            for k in range(n_depth)
-        ]
-        for y in range(n_y)
-    ]
-    place = (lax.axis_index("dom") // n_core % n_y) * n_bucket + lax.axis_index("bucket")
-    return along, across, place
+    outside = [(y, high) for y in range(n_y) for high in range(n_z // near)]
+    along = [[device(x, y, c, high, low, k) for x, c, low, k in inside] for y, high in outside]
+    across = [[device(x, y, c, high, low, k) for y, high in outside] for x, c, low, k in inside]
+    dom = lax.axis_index("dom")
+    place = dom // (n_y * n_core) * n_core + dom % n_core
+    place = place * near + lax.axis_index("bucket") % near
+    return along, across, place * n_k + lax.axis_index("depth")
 
 
 def local(
@@ -354,10 +355,10 @@
     groups = len(along[0])
     share = n_rel // groups
 
-    def exchange(pieces, axis, index_groups):
-        return lax.all_to_all(pieces, axis, 0, 0, axis_index_groups=index_groups)
-
-    pieces = exchange(rel_grad.reshape(groups, share, width), ("dom", "bucket"), along)
+    def exchange(pieces, index_groups):
+        return lax.all_to_all(pieces, AXES, 0, 0, axis_index_groups=index_groups)
+
+    pieces = exchange(rel_grad.reshape(groups, share, width), along)
 
     far_grad, grad_b = call(
         other_block,
@@ -383,10 +384,10 @@
     pieces, far_grad = lax.optimization_barrier((pieces, far_grad))
     stack = (shape((len(across[0]), share, width), F32),)
     (partial,) = call(sum_spread, (pieces,), stack, "v", "b")
-    totals = exchange(partial, ("dom", "depth"), across)
+    totals = exchange(partial, across)
     stack = (shape((groups, share, width), F32),)
     (new_rel,) = call(update_relations, (totals, my_rel, my_state), stack, "vvv", "b")
-    new_relations = exchange(new_rel, ("dom", "bucket"), along).reshape(n_rel, width)
+    new_relations = exchange(new_rel, along).reshape(n_rel, width)
 
     new_state, new_entities = call(
         update_entities,

time: 102 us -> 97.7 us (0.958)
  the two profiles are of different devices: /device:TPU:8 before, /device:TPU:40 now
where the time goes in v2:
time: 97.7 us; the launch traced here: 97.1 us
  starting transfers between devices  44.5 us (46%)
  waiting for transfers between devices  27.1 us (28%)
  Pallas kernels  22.6 us (23%)
  between operations  1.52 us (2%)
  local copies, waits for them, and re-layouts  1.34 us (1%)
    all_to_all x3, starting transfers between devices, exchange(): return lax.all_to_all(pieces, AXES, 0, 0, axis_index_groups=index_groups)  28.5 us
    pallas_call x7, Pallas kernels, call(): pl.pallas_call(kernel, out_shape=[pltpu.HBM(out.shape, out.dtype) if spac...  22.6 us
    ppermute x5, waiting for transfers between devices, passed_along(): lax.ppermute(block, axis, [((i - distance) % size, i) for i in range(size)])  16.4 us
    ppermute x5, starting transfers between devices, passed_along(): lax.ppermute(block, axis, [((i - distance) % size, i) for i in range(size)])  16 us
    all_to_all x3, waiting for transfers between devices, exchange(): return lax.all_to_all(pieces, AXES, 0, 0, axis_index_groups=index_groups)  10.7 us
  transfers between devices with their start and end apart: 8, of which 5 were waited for; matrix products, arithmetic and copies ran while one was open for 0% of the time, Pallas kernels for 16%

profile of v2, /device:TPU:40, one launch (start us, length us, event | category | flops | bytes accessed | tf_op | source)
XLA Modules:
  0.0 97.1 jit_solution(16920937035204967528)
XLA Ops:
  0.6 0.0 copy-start
  0.6 0.0 copy-start.6
  0.7 0.0 copy-start.5
  0.7 0.0 copy-start.4
  0.7 1.4 %shard_map.103 = (bf16[400,256]{1,0:T(8,128)(2,1)S(1)}, bf16[400,512]{1,0:T(8,128)(2,1)S(1)}, bf16[400,1024]{1,0:T(8,128)(2,1)S(1)}) custom-call(s32[1]{0:T(128)} %bitcast.depth.block, f32[400,1024]{1,0:T(8,128)} %bitcast.14), custom_call_target="tpu_custom_call" | custom-call | tf_op jit(solution)/shard_map/pallas_call | solution.py:251
  2.1 4.9 %collective-permute-start = (bf16[400,256]{1,0:T(8,128)(2,1)S(1)}, bf16[400,256]{1,0:T(8,128)(2,1)S(1)}, u32[]{:S(2)}, u32[]{:S(2)}) collective-permute-start(bf16[400,256]{1,0:T(8,128)(2,1)S(1)} %get-tuple-element.23), channel_id=1, source_target_pairs={{256,0},{272,16},{288,32},{304,48},{320,64},{336,80},{352,96},{368... | collective-permute-start | bytes 614408 | tf_op jit(solution)/shard_map/ppermute | solution.py:266
  7.1 2.4 %collective-permute-start.1 = (bf16[400,512]{1,0:T(8,128)(2,1)S(1)}, bf16[400,512]{1,0:T(8,128)(2,1)S(1)}, u32[]{:S(2)}, u32[]{:S(2)}) collective-permute-start(bf16[400,512]{1,0:T(8,128)(2,1)S(1)} %get-tuple-element.25), channel_id=1, source_target_pairs={{256,0},{272,16},{288,32},{304,48},{320,64},{336,80},{352,96},{368... | collective-permute-start | bytes 1228808 | tf_op jit(solution)/shard_map/ppermute | solution.py:266
  9.5 3.0 %collective-permute-done.outer = bf16[400,256]{1,0:T(8,128)(2,1)S(1)} collective-permute-done((bf16[400,256]{1,0:T(8,128)(2,1)S(1)}, bf16[400,256]{1,0:T(8,128)(2,1)S(1)}, u32[]{:S(2)}, u32[]{:S(2)}) %collective-permute-start) | collective-permute-done | bytes 204832 | tf_op jit(solution)/shard_map/ppermute | solution.py:266
  12.5 3.2 %collective-permute-start.2 = (bf16[400,256]{1,0:T(8,128)(2,1)S(1)}, bf16[400,256]{1,0:T(8,128)(2,1)S(1)}, u32[]{:S(2)}, u32[]{:S(2)}) collective-permute-start(bf16[400,256]{1,0:T(8,128)(2,1)S(1)} %collective-permute-done.outer), channel_id=1, source_target_pairs={{1,0},{0,1},{3,2},{2,3},{5,4},{4,5},{7,6},{6,7},{9,8},{8,9},{11,10... | collective-permute-start | bytes 614408 | tf_op jit(solution)/shard_map/ppermute | solution.py:266
  15.8 0.0 copy-done.6
  15.8 2.6 %collective-permute-start.3 = (s32[2,512]{1,0:T(2,128)S(1)}, s32[2,512]{1,0:T(2,128)S(1)}, u32[]{:S(2)}, u32[]{:S(2)}) collective-permute-start(s32[2,512]{1,0:T(2,128)S(1)} %copy-done.6), channel_id=1, source_target_pairs={{1,0},{0,1},{3,2},{2,3},{5,4},{4,5},{7,6},{6,7},{9,8},{8,9},{11,10... | collective-permute-start | bytes 12296 | tf_op jit(solution)/shard_map/ppermute | solution.py:266
  19.0 2.3 %collective-permute-done.3.neg_b = s32[2,512]{1,0:T(2,128)S(1)} collective-permute-done((s32[2,512]{1,0:T(2,128)S(1)}, s32[2,512]{1,0:T(2,128)S(1)}, u32[]{:S(2)}, u32[]{:S(2)}) %collective-permute-start.3) | collective-permute-done | bytes 4128 | tf_op jit(solution)/shard_map/ppermute | solution.py:266
  21.3 0.0 copy-done.5
  21.3 0.0 copy-done.4
  21.3 3.0 %shard_map.104 = (bf16[400,1024]{1,0:T(8,128)(2,1)S(1)}, bf16[400,1024]{1,0:T(8,128)(2,1)S(1)}, f32[400,1024]{1,0:T(8,128)S(1)}, f32[2,1024,128]{2,1,0:T(8,128)S(1)}) custom-call(bf16[400,1024]{1,0:T(8,128)(2,1)S(1)} %get-tuple-element.26.own, s32[2,1024]{1,0:T(2,128)S(1)} %copy-done.4, s32[1,1024]{1,0:T(1,128)S(1)} %bitcast.11, s32[2,512]{1,0:T(2,128)S(1)} %copy-done.6, ...), custom_call_target="tpu_custom_call" | custom-call | tf_op jit(solution)/shard_map/pallas_call | solution.py:251
  24.3 0.0 copy-start.1
  24.3 0.0 copy-start.2
  24.3 0.0 copy-start.3
  24.3 0.0 collective-permute-done.2.peer
  24.3 0.0 collective-permute-done.1.middle
  24.3 4.6 %shard_map.105 = (bf16[1024,512]{1,0:T(8,128)(2,1)}, bf16[1024,512]{1,0:T(8,128)(2,1)}, bf16[400,512]{1,0:T(8,128)(2,1)}, f32[256,400]{1,0:T(8,128)}, bf16[400,1024]{1,0:T(8,128)(2,1)}) custom-call(s32[1]{0:T(128)} %bitcast.depth.block, s32[1]{0:T(128)S(6)} %copy.15.live, s32[2,1024]{1,0:T(2,128)S(1)} %copy-done.4, s32[1,1024]{1,0:T(1,128)S(1)} %bitcast.12, ...), custom_call_target="tpu_custom_call" | custom-call | tf_op jit(solution)/shard_map/pallas_call | solution.py:251
  29.0 0.0 copy-done.1
  29.0 0.0 copy-done.2
  29.0 0.0 copy-done.3
  29.0 8.7 %all-to-all-start = ((f32[32,8,400]{2,1,0:T(8,128)}), f32[32,8,400]{2,1,0:T(8,128)S(1)}, u32[]{:S(2)}, u32[]{:S(2)}) async-start(f32[32,8,400]{2,1,0:T(8,128)} %bitcast.18), calls=%async_computation | async-start | bytes 1048576 | tf_op jit(solution)/shard_map/all_to_all | solution.py:359
  37.7 0.0 copy-start.8
  37.7 7.1 %shard_map.106 = (bf16[400,1024]{1,0:T(8,128)(2,1)S(1)}, bf16[400,512]{1,0:T(8,128)(2,1)}) custom-call(s32[1]{0:T(128)} %bitcast.depth.block, s32[1]{0:T(128)S(6)} %copy.15.live, s32[2,1024]{1,0:T(2,128)S(1)} %copy-done.4, bf16[400,1024]{1,0:T(8,128)(2,1)} %get-tuple-element.31.far_hbm, bf16[400,1024]{1,0:T(8,128)(2,1)} %copy-done.3, f32[400,1024]{1,0:T(8,128)} %copy-done.1, ...), custom_call_target="tpu_custom_call" | custom-call | tf_op jit(solution)/shard_map/pallas_call | solution.py:251
  44.8 2.7 %all-to-all-done.pieces = f32[32,8,400]{2,1,0:T(8,128)S(1)} async-done(((f32[32,8,400]{2,1,0:T(8,128)}), f32[32,8,400]{2,1,0:T(8,128)S(1)}, u32[]{:S(2)}, u32[]{:S(2)}) %all-to-all-start) | async-done | bytes 409632 | tf_op jit(solution)/shard_map/all_to_all | solution.py:359
  47.5 0.8 shard_map.108
  48.3 0.0 copy-start.7
  48.3 14.9 %all-to-all-start.1 = ((f32[16,8,400]{2,1,0:T(8,128)}), f32[16,8,400]{2,1,0:T(8,128)S(1)}, u32[]{:S(2)}, u32[]{:S(2)}) async-start(f32[16,8,400]{2,1,0:T(8,128)} %shard_map.108), calls=%async_computation.1 | async-start | bytes 524288 | tf_op jit(solution)/shard_map/all_to_all | solution.py:359
  63.2 0.0 copy-done.8
  63.2 0.1 constant_dynamic-slice_fusion
  63.3 2.9 %collective-permute-start.4 = (bf16[400,1024]{1,0:T(8,128)(2,1)S(1)}, bf16[400,1024]{1,0:T(8,128)(2,1)S(1)}, u32[]{:S(2)}, u32[]{:S(2)}) collective-permute-start(bf16[400,1024]{1,0:T(8,128)(2,1)S(1)} %get-tuple-element.34), channel_id=1, source_target_pairs={{256,0},{272,16},{288,32},{304,48},{320,64},{336,80},{352,96},{368... | collective-permute-start | bytes 2457608 | tf_op jit(solution)/shard_map/ppermute | solution.py:266
  66.2 0.0 copy-done
  66.2 0.1 dynamic-slice_bitcast_fusion
  66.3 0.1 copy.14.rel
  66.4 0.1 copy.12.state
  66.5 8.0 %all-to-all-done.1.pieces = f32[16,8,400]{2,1,0:T(8,128)S(1)} async-done(((f32[16,8,400]{2,1,0:T(8,128)}), f32[16,8,400]{2,1,0:T(8,128)S(1)}, u32[]{:S(2)}, u32[]{:S(2)}) %all-to-all-start.1) | async-done | bytes 204832 | tf_op jit(solution)/shard_map/all_to_all | solution.py:359
  74.4 1.0 %shard_map.109 = f32[32,8,400]{2,1,0:T(8,128)} custom-call(f32[16,8,400]{2,1,0:T(8,128)S(1)} %all-to-all-done.1.pieces, f32[8,400]{1,0:T(8,128)S(1)} %copy.14.rel, f32[8,1]{1,0:T(8,128)S(1)} %copy.12.state), custom_call_target="tpu_custom_call" | custom-call | tf_op jit(solution)/shard_map/pallas_call | solution.py:251
  75.5 4.9 %all-to-all-start.2 = ((f32[32,8,400]{2,1,0:T(8,128)}), f32[32,8,400]{2,1,0:T(8,128)S(1)}, u32[]{:S(2)}, u32[]{:S(2)}) async-start(f32[32,8,400]{2,1,0:T(8,128)} %shard_map.109), calls=%async_computation.2 | async-start | bytes 1048576 | tf_op jit(solution)/shard_map/all_to_all | solution.py:359
  80.4 11.1 %collective-permute-done.4.home = bf16[400,1024]{1,0:T(8,128)(2,1)S(1)} collective-permute-done((bf16[400,1024]{1,0:T(8,128)(2,1)S(1)}, bf16[400,1024]{1,0:T(8,128)(2,1)S(1)}, u32[]{:S(2)}, u32[]{:S(2)}) %collective-permute-start.4) | collective-permute-done | bytes 819232 | tf_op jit(solution)/shard_map/ppermute | solution.py:266
  91.5 0.0 copy-done.7
  91.5 4.6 %shard_map.107 = (f32[1,1024]{1,0:T(1,128)}, f32[400,1024]{1,0:T(8,128)}) custom-call(s32[1]{0:T(128)} %bitcast.depth.block, s32[2,1024]{1,0:T(2,128)S(1)} %copy-done.4, f32[1,1024]{1,0:T(1,128)S(1)} %bitcast.13, bf16[400,1024]{1,0:T(8,128)(2,1)S(1)} %collective-permute-done.4.home, f32[400,1024]{1,0:T(8,128)} %bitcast.15, ...), custom_call_target="tpu_custom_call" | custom-call | tf_op jit(solution)/shard_map/pallas_call | solution.py:251
  96.1 0.0 all-to-all-done.2
  96.1 0.9 copy.13
Async XLA Ops:
  0.6 65.6 %copy-start = (f32[256]{0:T(256)S(1)}, f32[256]{0:T(256)}, u32[]{:S(2)}) copy-start(f32[256]{0:T(256)} %param.11) | copy-start | bytes 3076
  0.6 15.1 %copy-start.6 = (s32[2,512]{1,0:T(2,128)S(1)}, s32[2,512]{1,0:T(2,128)}, u32[]{:S(2)}) copy-start(s32[2,512]{1,0:T(2,128)} %neg_a.1) | copy-start | bytes 12292
  0.7 20.6 %copy-start.5 = (s32[1024]{0:T(1024)S(1)}, s32[1024]{0:T(1024)}, u32[]{:S(2)}) copy-start(s32[1024]{0:T(1024)} %param.13) | copy-start | bytes 12292
  0.7 20.6 %copy-start.4 = (s32[2,1024]{1,0:T(2,128)S(1)}, s32[2,1024]{1,0:T(2,128)}, u32[]{:S(2)}) copy-start(s32[2,1024]{1,0:T(2,128)} %ends.7) | copy-start | bytes 24580
  2.1 10.4 %collective-permute-start = (bf16[400,256]{1,0:T(8,128)(2,1)S(1)}, bf16[400,256]{1,0:T(8,128)(2,1)S(1)}, u32[]{:S(2)}, u32[]{:S(2)}) collective-permute-start(bf16[400,256]{1,0:T(8,128)(2,1)S(1)} %get-tuple-element.23), channel_id=1, source_target_pairs={{256,0},{272,16},{288,32},{304,48},{320,64},{336,80},{352,96},{368... | collective-permute-start | bytes 614408 | tf_op jit(solution)/shard_map/ppermute | solution.py:266
  7.1 17.3 %collective-permute-start.1 = (bf16[400,512]{1,0:T(8,128)(2,1)S(1)}, bf16[400,512]{1,0:T(8,128)(2,1)S(1)}, u32[]{:S(2)}, u32[]{:S(2)}) collective-permute-start(bf16[400,512]{1,0:T(8,128)(2,1)S(1)} %get-tuple-element.25), channel_id=1, source_target_pairs={{256,0},{272,16},{288,32},{304,48},{320,64},{336,80},{352,96},{368... | collective-permute-start | bytes 1228808 | tf_op jit(solution)/shard_map/ppermute | solution.py:266
  12.5 11.8 %collective-permute-start.2 = (bf16[400,256]{1,0:T(8,128)(2,1)S(1)}, bf16[400,256]{1,0:T(8,128)(2,1)S(1)}, u32[]{:S(2)}, u32[]{:S(2)}) collective-permute-start(bf16[400,256]{1,0:T(8,128)(2,1)S(1)} %collective-permute-done.outer), channel_id=1, source_target_pairs={{1,0},{0,1},{3,2},{2,3},{5,4},{4,5},{7,6},{6,7},{9,8},{8,9},{11,10... | collective-permute-start | bytes 614408 | tf_op jit(solution)/shard_map/ppermute | solution.py:266
  15.8 5.5 %collective-permute-start.3 = (s32[2,512]{1,0:T(2,128)S(1)}, s32[2,512]{1,0:T(2,128)S(1)}, u32[]{:S(2)}, u32[]{:S(2)}) collective-permute-start(s32[2,512]{1,0:T(2,128)S(1)} %copy-done.6), channel_id=1, source_target_pairs={{1,0},{0,1},{3,2},{2,3},{5,4},{4,5},{7,6},{6,7},{9,8},{8,9},{11,10... | collective-permute-start | bytes 12296 | tf_op jit(solution)/shard_map/ppermute | solution.py:266
  24.3 4.7 %copy-start.1 = (f32[400,1024]{1,0:T(8,128)}, f32[400,1024]{1,0:T(8,128)S(1)}, u32[]{:S(2)}) copy-start(f32[400,1024]{1,0:T(8,128)S(1)} %get-tuple-element.29.scale.scale_hbm) | copy-start | bytes 4915204
  24.3 4.7 %copy-start.2 = (f32[2,1024,128]{2,1,0:T(8,128)}, f32[2,1024,128]{2,1,0:T(8,128)S(1)}, u32[]{:S(2)}) copy-start(f32[2,1024,128]{2,1,0:T(8,128)S(1)} %get-tuple-element.30.count.count_hbm) | copy-start | bytes 3145732
  24.3 4.7 %copy-start.3 = (bf16[400,1024]{1,0:T(8,128)(2,1)}, bf16[400,1024]{1,0:T(8,128)(2,1)S(1)}, u32[]{:S(2)}) copy-start(bf16[400,1024]{1,0:T(8,128)(2,1)S(1)} %get-tuple-element.27.q.q_hbm) | copy-start | bytes 2457604
  29.0 18.5 %all-to-all-start = ((f32[32,8,400]{2,1,0:T(8,128)}), f32[32,8,400]{2,1,0:T(8,128)S(1)}, u32[]{:S(2)}, u32[]{:S(2)}) async-start(f32[32,8,400]{2,1,0:T(8,128)} %bitcast.18), calls=%async_computation | async-start | bytes 1048576 | tf_op jit(solution)/shard_map/all_to_all | solution.py:359
  37.7 25.5 %copy-start.8 = (f32[256,400]{0,1:T(8,128)S(1)}, f32[256,400]{0,1:T(8,128)}, u32[]{:S(2)}) copy-start(f32[256,400]{0,1:T(8,128)} %param.10) | copy-start | bytes 1228804
  48.3 43.2 %copy-start.7 = (f32[1024]{0:T(1024)S(1)}, f32[1024]{0:T(1024)}, u32[]{:S(2)}) copy-start(f32[1024]{0:T(1024)} %param.9) | copy-start | bytes 12292
  48.3 26.2 %all-to-all-start.1 = ((f32[16,8,400]{2,1,0:T(8,128)}), f32[16,8,400]{2,1,0:T(8,128)S(1)}, u32[]{:S(2)}, u32[]{:S(2)}) async-start(f32[16,8,400]{2,1,0:T(8,128)} %shard_map.108), calls=%async_computation.1 | async-start | bytes 524288 | tf_op jit(solution)/shard_map/all_to_all | solution.py:359
  63.3 28.2 %collective-permute-start.4 = (bf16[400,1024]{1,0:T(8,128)(2,1)S(1)}, bf16[400,1024]{1,0:T(8,128)(2,1)S(1)}, u32[]{:S(2)}, u32[]{:S(2)}) collective-permute-start(bf16[400,1024]{1,0:T(8,128)(2,1)S(1)} %get-tuple-element.34), channel_id=1, source_target_pairs={{256,0},{272,16},{288,32},{304,48},{320,64},{336,80},{352,96},{368... | collective-permute-start | bytes 2457608 | tf_op jit(solution)/shard_map/ppermute | solution.py:266
  75.5 20.6 %all-to-all-start.2 = ((f32[32,8,400]{2,1,0:T(8,128)}), f32[32,8,400]{2,1,0:T(8,128)S(1)}, u32[]{:S(2)}, u32[]{:S(2)}) async-start(f32[32,8,400]{2,1,0:T(8,128)} %shard_map.109), calls=%async_computation.2 | async-start | bytes 1048576 | tf_op jit(solution)/shard_map/all_to_all | solution.py:359
